TPU v7x, 256 devices: a whole 4x4x8 slice. The times are simulated.
256 devices in a mesh: gx: 32 (over y, x, core), gy: 8 (over z).
Axes of the slice: x: 4, y: 4, z: 8, core: 2. Of those that a mesh axis runs over, the one named last changes fastest.
Arguments:
- displacement: float32 [3, 32, 256, 1024], P(None, None, 'gx', 'gy'), may hold values from -6 to 6
- velocity: float32 [3, 32, 256, 1024], P(None, None, 'gx', 'gy'), may hold values from -6 to 6
- slopes: float32 [2, 32, 256, 1024], P(None, None, 'gx', 'gy'), may hold values from -0.5 to 0.5
- stretch: float32 [32, 256, 1024], P(None, 'gx', 'gy'), may hold values from 0.6 to 1.4
- moduli: float32 [2, 32, 256, 1024], P(None, None, 'gx', 'gy'), may hold values from 0.3 to 1
- buoyancy: float32 [32, 256, 1024], P(None, 'gx', 'gy'), may hold values from 0.5 to 1.5
- probes: float32 [4, 512, 128], P(None, 'gy'), may hold values from -0.0017089844 to 0.0017089844
Outputs:
- final_displacement: float32 [3, 32, 256, 1024], P(None, None, 'gx', 'gy')
- basis: float32 [128, 48, 128], P('gx', 'gy')
- factor: float32 [128, 128], replicated
All inputs are finite; a program needn't handle non-finite values.
Results may differ from a plain program's by a relative error of at most 0.0003.
Values sent between devices are 32-bit elements; how exact they have to be, the bound alone decides.
A program may use at most 64 MiB of HBM per device.

v0:
```python
import math
import jax
import jax.numpy as jnp
from jax import lax
from jax.sharding import PartitionSpec as P

STEPS = 4
time_step = 0.12


def extended(block, sides, width):
    for axis, dim in sides:
        count = lax.axis_size(axis)
        forward = [(i, i + 1) for i in range(count - 1)]
        backward = [(target, source) for source, target in forward]
        low = lax.ppermute(
            lax.slice_in_dim(block, block.shape[dim] - width, None, axis=dim), axis, forward
        )
        high = lax.ppermute(lax.slice_in_dim(block, 0, width, axis=dim), axis, backward)
        block = jnp.concatenate([low, block, high], axis=dim)
    return block


def fourth(values, dimension):
    length_out = values.shape[dimension] - 4

    def segment(offset):
        return lax.slice_in_dim(values, offset, offset + length_out, axis=dimension)

    return (segment(0) - segment(4) + 8.0 * (segment(3) - segment(1))) / 12.0


def vertical(values):
    padded = jnp.pad(values, ((0, 0), (2, 2), (0, 0), (0, 0)))
    return fourth(padded, 1)


def gradient(padded, slope_x, slope_y, stretch):
    d_x = fourth(padded[:, :, :, 2:-2], 2)
    d_y = fourth(padded[:, :, 2:-2, :], 3)
    d_r = vertical(padded[:, :, 2:-2, 2:-2])
    return jnp.stack([d_x + slope_x * d_r, d_y + slope_y * d_r, stretch * d_r], axis=1)


def stresses(gradients, lame, shear):
    divergence = gradients[0, 0] + gradients[1, 1] + gradients[2, 2]
    pressure = lame * divergence
    return jnp.stack(
        [
            pressure + 2.0 * shear * gradients[0, 0],
            pressure + 2.0 * shear * gradients[1, 1],
            pressure + 2.0 * shear * gradients[2, 2],
            shear * (gradients[0, 1] + gradients[1, 0]),
            shear * (gradients[0, 2] + gradients[2, 0]),
            shear * (gradients[1, 2] + gradients[2, 1]),
        ]
    )


def forces(padded, slope_x, slope_y, stretch):
    d_x = fourth(padded[:, :, :, 2:-2], 2)
    d_y = fourth(padded[:, :, 2:-2, :], 3)
    d_r = vertical(padded[:, :, 2:-2, 2:-2])
    rows_x = (0, 3, 4)
    rows_y = (3, 1, 5)
    rows_z = (4, 5, 2)
    return jnp.stack(
        [
            d_x[rows_x[component]]
            + slope_x * d_r[rows_x[component]]
            + d_y[rows_y[component]]
            + slope_y * d_r[rows_y[component]]
            + stretch * d_r[rows_z[component]]
            for component in range(3)
        ]
    )


def lower_factor(gram):
    order = gram.shape[0]
    positions = jnp.arange(order, dtype=jnp.int32)

    def column_step(column_index, lower):
        picker = (positions == column_index).astype(jnp.float32)
        column = jnp.dot(gram, picker, precision=lax.Precision.HIGHEST)
        row_of = jnp.dot(picker, lower, precision=lax.Precision.HIGHEST)
        column = column - jnp.dot(lower, row_of, precision=lax.Precision.HIGHEST)
        pivot = jnp.sqrt(jnp.sum(column * picker))
        entries = jnp.where(
            positions > column_index,
            column / pivot,
            jnp.where(positions == column_index, pivot, 0.0),
        )
        return lower + entries[:, None] * picker[None, :]

    return lax.fori_loop(0, order, column_step, jnp.zeros_like(gram))


def lower_inverse(lower):
    order = lower.shape[0]
    positions = jnp.arange(order, dtype=jnp.int32)

    def row_step(row_index, inverse):
        picker = (positions == row_index).astype(jnp.float32)
        row_of = jnp.dot(picker, lower, precision=lax.Precision.HIGHEST)
        pivot = jnp.sum(row_of * picker)
        fresh = (picker - jnp.dot(row_of, inverse, precision=lax.Precision.HIGHEST)) / pivot
        return inverse + picker[:, None] * fresh[None, :]

    return lax.fori_loop(0, order, row_step, jnp.zeros_like(lower))


def orthogonalize(tall_block, gram):
    lower = lower_factor(gram)
    inverse = lower_inverse(lower)
    result = jnp.dot(
        tall_block, inverse.T, precision=lax.Precision.HIGHEST, preferred_element_type=jnp.float32
    )
    return (result, lower.T)


def shards(displacement, velocity, slopes, stretch, moduli, buoyancy, probes):
    previous = displacement - time_step * velocity
    current = displacement
    for moment in range(STEPS):
        padded = extended(current, (("gx", 2), ("gy", 3)), 2)
        gradients = gradient(padded, slopes[0], slopes[1], stretch)
        stress = extended(stresses(gradients, moduli[0], moduli[1]), (("gx", 2), ("gy", 3)), 2)
        pushes = buoyancy * forces(stress, slopes[0], slopes[1], stretch)
        following = 2.0 * current - previous + time_step**2 * pushes
        velocities = (following - previous) / (2.0 * time_step)
        sampled = velocities[:, ::2, ::2, ::2]
        half_x = sampled.shape[2]
        rearranged = jnp.transpose(sampled, (2, 0, 1, 3)).reshape(-1, sampled.shape[3])
        sketch_term = jnp.dot(
            rearranged,
            probes[moment],
            precision=lax.Precision.HIGHEST,
            preferred_element_type=jnp.float32,
        ).reshape(half_x, -1, probes.shape[2])
        reduced = lax.psum_scatter(sketch_term, "gy", scatter_dimension=1, tiled=True)
        sketch = reduced if moment == 0 else sketch + reduced
        previous, current = (current, following)
    tall_block = sketch.reshape(-1, sketch.shape[2])
    rows_total = tall_block.shape[0] * lax.axis_size("gx") * lax.axis_size("gy")
    gram_local = jnp.dot(
        tall_block.T,
        tall_block,
        precision=lax.Precision.HIGHEST,
        preferred_element_type=jnp.float32,
    )
    gram_whole = lax.psum(gram_local, ("gx", "gy"))
    orthonormal, factor = orthogonalize(tall_block, gram_whole)
    basis = (math.sqrt(rows_total) * orthonormal).reshape(sketch.shape)
    return (current, basis, factor)


def solution(mesh):
    in_specs = (
        P(None, None, "gx", "gy"),
        P(None, None, "gx", "gy"),
        P(None, None, "gx", "gy"),
        P(None, "gx", "gy"),
        P(None, None, "gx", "gy"),
        P(None, "gx", "gy"),
        P(None, "gy", None),
    )
    out_specs = (P(None, None, "gx", "gy"), P("gx", "gy", None), P())
    return jax.shard_map(shards, mesh=mesh, in_specs=in_specs, out_specs=out_specs, check_vma=False)
```

profile of v0, /device:TPU:1, one launch (start us, length us, event | category | flops | bytes accessed | tf_op | source)
XLA Modules:
  0.0 1194.3 jit_solution(5939340690643367252)
XLA Ops:
  8.8 4.6 collective-permute-start
  18.1 4.4 collective-permute-done.1
  26.6 4.9 collective-permute-start.2
  35.1 3.8 fusion.119
  49.6 4.4 collective-permute-done.5
  59.1 3.6 collective-permute-start.6
  76.9 3.5 collective-permute-start.8
  82.4 4.0 collective-permute-done.9
  89.0 3.7 collective-permute-start.10
  107.4 4.4 collective-permute-done.13
  117.2 5.1 collective-permute-start.14
  141.4 6.0 slice.1072
  150.9 3.6 collective-permute-start.18
  163.3 5.1 collective-permute-start.20
  171.9 6.0 slice.1074
  185.3 3.9 collective-permute-start.22
  202.2 5.1 collective-permute-start.24
  225.0 5.1 collective-permute-start.28
  233.0 4.0 collective-permute-done.29
  243.1 3.7 collective-permute-start.30
  266.5 78.0 %all-reduce.14.cloned.1.call-done = f32[4,48,128]{2,0,1:T(4,128)} async-done(((f32[4,48,128]{2,0,1:T(4,128)}), f32[4,48,128]{2,0,1:T(4,128)}) %all-reduce.14.cloned.1.call-update) | async-done | bytes 98320
  347.2 245.3 %all-reduce.12.cloned.1.call-done = f32[128,128]{1,0:T(8,128)} async-done(((f32[128,128]{1,0:T(8,128)}), f32[128,128]{1,0:T(8,128)}) %all-reduce.12.cloned.1.call-update) | async-done | bytes 65552 | tf_op jit(solution)/shard_map/psum | solution.py:152
  592.5 363.3 %while.30 = (s32[]{:T(128)}, f32[128,128]{1,0:T(8,128)S(1)}, f32[128,128]{1,0:T(8,128)}, s32[]{:T(128)}, s32[]{:T(128)}) while((s32[]{:T(128)}, f32[128,128]{1,0:T(8,128)S(1)}, f32[128,128]{1,0:T(8,128)}, s32[]{:T(128)}, s32[]{:T(128)}) %tuple.125), condition=%wide.region_7.8_spmd.clone.clone, body=%wide.region_5.7_spmd.clone.clone.sunk | while | flops 673410 | bytes 332917 | solution.py:96
  956.5 230.0 %while.29 = (s32[]{:T(128)}, f32[128,128]{1,0:T(8,128)S(1)}, f32[128,128]{1,0:T(8,128)S(1)}, s32[]{:T(128)}, s32[]{:T(128)}) while((s32[]{:T(128)}, f32[128,128]{1,0:T(8,128)S(1)}, f32[128,128]{1,0:T(8,128)S(1)}, s32[]{:T(128)}, s32[]{:T(128)}) %tuple.128), condition=%wide.region_10.11_spmd.clone, body=%wide.region_8.10_spmd.clone.sunk | while | flops 460034 | bytes 265316 | solution.py:110
  (1549 shorter events, 667.7 us)
Async XLA Ops:
  7.2 337.4 %all-reduce.14.cloned.1.call-start = ((), (), s32[]{:S(2)}) async-start(), calls=%async_computation.1 | async-start | bytes 196608
  8.8 9.3 collective-permute-start
  13.4 9.1 collective-permute-start.1
  25.3 16.2 %collective-permute-start.3 = (f32[3,32,12,2]{1,3,2,0:T(2,128)}, f32[3,32,12,2]{1,3,2,0:T(2,128)}, u32[]{:S(2)}, u32[]{:S(2)}) collective-permute-start(f32[3,32,12,2]{1,3,2,0:T(2,128)} %get-tuple-element.276), channel_id=1, source_target_pairs={{1,0},{2,1},{3,2},{4,3},{5,4},{6,5},{7,6},{9,8},{10,9},{11,10},{12... | collective-permute-start | bytes 27656 | tf_op jit(solution)/shard_map/ppermute | solution.py:19
  26.6 13.8 %collective-permute-start.2 = (f32[3,32,12,2]{1,3,2,0:T(2,128)}, f32[3,32,12,2]{1,3,2,0:T(2,128)}, u32[]{:S(2)}, u32[]{:S(2)}) collective-permute-start(f32[3,32,12,2]{1,3,2,0:T(2,128)} %get-tuple-element.277), channel_id=1, source_target_pairs={{0,1},{1,2},{2,3},{3,4},{4,5},{5,6},{6,7},{8,9},{9,10},{10,11},{11... | collective-permute-start | bytes 27656 | tf_op jit(solution)/shard_map/ppermute | solution.py:16
  47.0 7.0 collective-permute-start.5
  59.1 10.4 collective-permute-start.6
  80.4 5.9 collective-permute-start.9
  89.0 9.1 collective-permute-start.10
  104.8 7.0 collective-permute-start.13
  117.2 13.2 %collective-permute-start.14 = (f32[6,32,12,2]{1,3,2,0:T(2,128)S(1)}, f32[6,32,12,2]{1,3,2,0:T(2,128)S(1)}, u32[]{:S(2)}, u32[]{:S(2)}) collective-permute-start(f32[6,32,12,2]{1,3,2,0:T(2,128)S(1)} %copy.329), channel_id=1, source_target_pairs={{0,1},{1,2},{2,3},{3,4},{4,5},{5,6},{6,7},{8,9},{9,10},{10,11},{11... | collective-permute-start | bytes 55304 | tf_op jit(solution)/shard_map/ppermute | solution.py:16
  136.6 11.5 collective-permute-start.16
  139.5 8.6 collective-permute-start.17
  150.9 8.8 collective-permute-start.18
  163.3 15.3 %collective-permute-start.20 = (f32[6,32,2,128]{3,1,2,0:T(8,128)S(1)}, f32[6,32,2,128]{3,1,2,0:T(8,128)S(1)}, u32[]{:S(2)}, u32[]{:S(2)}) collective-permute-start(f32[6,32,2,128]{3,1,2,0:T(8,128)S(1)} %get-tuple-element.294), channel_id=1, source_target_pairs={{0,8},{8,16},{16,24},{24,32},{32,40},{40,48},{48,56},{56,64},{64,7... | collective-permute-start | bytes 589832 | tf_op jit(solution)/shard_map/ppermute | solution.py:16
  168.4 10.2 collective-permute-start.21
  185.3 11.0 collective-permute-start.22
  202.2 11.8 collective-permute-start.24
  207.3 6.7 collective-permute-start.25
  214.9 7.5 collective-permute-start.26
  225.0 8.0 collective-permute-start.28
  230.1 7.0 collective-permute-start.29
  243.1 11.6 collective-permute-start.30
  265.2 327.3 %all-reduce.12.cloned.1.call-start = ((), (), s32[]{:S(2)}) async-start(), calls=%async_computation | async-start | bytes 131072 | tf_op jit(solution)/shard_map/psum | solution.py:152
  (52 other events, 254.3 us)
Sparse Core Ops, SparseCore 0:
  265.3 79.1 all-reduce.13
  351.5 240.9 all-reduce.11
where the time goes:
time: 1210 us; the launch traced here: 1190 us
  matrix products  475 us (39%)
  waiting for transfers between devices  362 us (30%)
  loops' own time  98.3 us (8%)
  starting transfers between devices  89 us (7%)
  local copies, waits for them, and re-layouts  85.4 us (7%)
  other arithmetic  68.3 us (6%)
  between operations  15.9 us (1%)
    psum x1, waiting for transfers between devices, shards(): gram_whole = lax.psum(gram_local, ('gx', 'gy'))  245 us
    dot_general x128, matrix products, column_step(): column = jnp.dot(gram, picker, precision=lax.Precision.HIGHEST)  124 us
    dot_general x128, matrix products, column_step(): column = column - jnp.dot(lower, row_of, precision=lax.Precision.HIGHEST)  108 us
    dot_general x128, matrix products, row_step(): jnp.dot(row_of, inverse, precision=lax.Precision.HIGHEST)  107 us
    dot_general x128, matrix products, row_step(): row_of = jnp.dot(picker, lower, precision=lax.Precision.HIGHEST)  105 us
    another operation x1, loops' own time, lower_factor(): return lax.fori_loop(0, order, column_step, jnp.zeros_like(gram))  94 us
    unnamed x3, waiting for transfers between devices  78.1 us
    ppermute x16, starting transfers between devices, extended(): lax.ppermute(lax.slice_in_dim(block, block.shape[dim] - width, None, axis...  62.5 us
  transfers between devices with their start and end apart: 34, of which 17 were waited for; matrix products, arithmetic and copies ran while one was open for 5% of the time, Pallas kernels for 0%

commit v1 on v0

--- a/solution.py
+++ b/solution.py
@@ -149,7 +149,7 @@
         precision=lax.Precision.HIGHEST,
         preferred_element_type=jnp.float32,
     )
-    gram_whole = lax.psum(gram_local, ("gx", "gy"))
+    gram_whole = jnp.sum(lax.all_gather(gram_local, ("gx", "gy")), axis=0)
     orthonormal, factor = orthogonalize(tall_block, gram_whole)
     basis = (math.sqrt(rows_total) * orthonormal).reshape(sketch.shape)
     return (current, basis, factor)

time: 1210 us -> 966 us (0.80)
  matrix products: 475 us -> 352 us
  waiting for transfers between devices: 362 us -> 242 us
    psum x1 -> x0, waiting for transfers between devices: 245 us -> none  [shards(): gram_whole = lax.psum(gram_local, ('gx', 'gy'))]
    all_gather x0 -> x1, waiting for transfers between devices: none -> 130 us  [shards(): gram_whole = jnp.sum(lax.all_gather(gram_local, ('gx', 'gy')), axis=0)]
    dot_general x128, matrix products: 124 us -> 19 us  [column_step(): column = jnp.dot(gram, picker, precision=lax.Precision.HIGHEST)]
  transfers between devices with their start and end apart: 34 -> 34, of which waited for: 17 -> 16; matrix products, arithmetic and copies ran while one was open for 5% -> 6% of each run, Pallas kernels for 0% -> 0%
where the time goes in v1:
time: 966 us; the launch traced here: 960 us
  matrix products  352 us (36%)
  waiting for transfers between devices  242 us (25%)
  loops' own time  97.7 us (10%)
  starting transfers between devices  92.1 us (10%)
  local copies, waits for them, and re-layouts  86.6 us (9%)
  other arithmetic  73.9 us (8%)
  between operations  15.9 us (2%)
    all_gather x1, waiting for transfers between devices, shards(): gram_whole = jnp.sum(lax.all_gather(gram_local, ('gx', 'gy')), axis=0)  130 us
    dot_general x128, matrix products, column_step(): column = column - jnp.dot(lower, row_of, precision=lax.Precision.HIGHEST)  113 us
    dot_general x128, matrix products, row_step(): jnp.dot(row_of, inverse, precision=lax.Precision.HIGHEST)  98.2 us
    dot_general x128, matrix products, row_step(): row_of = jnp.dot(picker, lower, precision=lax.Precision.HIGHEST)  97.2 us
    another operation x1, loops' own time, lower_factor(): return lax.fori_loop(0, order, column_step, jnp.zeros_like(gram))  94 us
    unnamed x3, waiting for transfers between devices  79.7 us
    ppermute x16, starting transfers between devices, extended(): lax.ppermute(lax.slice_in_dim(block, block.shape[dim] - width, None, axis...  65.2 us
    ppermute x16, waiting for transfers between devices, extended(): lax.ppermute(lax.slice_in_dim(block, 0, width, axis=dim), axis, backward)  29.6 us
  transfers between devices with their start and end apart: 34, of which 16 were waited for; matrix products, arithmetic and copies ran while one was open for 6% of the time, Pallas kernels for 0%

profile of v1, /device:TPU:1, one launch (start us, length us, event | category | flops | bytes accessed | tf_op | source)
XLA Modules:
  0.0 959.9 jit_solution(8605386802294986912)
XLA Ops:
  8.8 4.6 collective-permute-start
  18.1 4.4 collective-permute-done.1
  25.3 4.1 collective-permute-start.2
  34.4 3.7 fusion.119
  48.7 4.4 collective-permute-done.5
  57.1 4.9 collective-permute-start.6
  81.4 4.0 collective-permute-done.9
  88.5 3.6 collective-permute-start.10
  108.0 4.4 collective-permute-done.13
  116.1 5.3 collective-permute-start.14
  140.5 6.0 slice.1072
  149.7 3.9 collective-permute-start.18
  162.7 6.1 collective-permute-start.20
  172.3 6.0 slice.1074
  184.4 3.9 collective-permute-start.22
  201.1 5.1 collective-permute-start.24
  213.5 3.7 collective-permute-start.26
  225.2 4.8 collective-permute-start.28
  240.7 3.6 collective-permute-start.30
  264.0 79.6 %all-reduce.11.cloned.1.call-done = f32[4,48,128]{2,0,1:T(4,128)} async-done(((f32[4,48,128]{2,0,1:T(4,128)}), f32[4,48,128]{2,0,1:T(4,128)}) %all-reduce.11.cloned.1.call-update) | async-done | bytes 98320
  346.3 130.4 %all-gather.3.cloned.1.call-done = f32[32768,128]{1,0:T(8,128)} async-done(((f32[128,128]{1,0:T(8,128)}), f32[32768,128]{1,0:T(8,128)}) %all-gather.3.cloned.1.call-update) | async-done | bytes 16777232 | tf_op jit(solution)/shard_map/all_gather | solution.py:152
  476.7 6.6 reduce_sum.35
  483.3 255.7 %while.30 = (s32[]{:T(128)}, f32[128,128]{1,0:T(8,128)S(1)}, f32[128,128]{1,0:T(8,128)S(1)}, s32[]{:T(128)}, s32[]{:T(128)}) while((s32[]{:T(128)}, f32[128,128]{1,0:T(8,128)S(1)}, f32[128,128]{1,0:T(8,128)S(1)}, s32[]{:T(128)}, s32[]{:T(128)}) %tuple.125), condition=%wide.region_7.8_spmd.clone.clone, body=%wide.region_5.7_spmd.clone.clone.sunk | while | flops 673410 | bytes 332909 | solution.py:96
  739.7 212.5 %while.29 = (s32[]{:T(128)}, f32[128,128]{1,0:T(8,128)S(1)}, f32[128,128]{1,0:T(8,128)S(1)}, s32[]{:T(128)}, s32[]{:T(128)}) while((s32[]{:T(128)}, f32[128,128]{1,0:T(8,128)S(1)}, f32[128,128]{1,0:T(8,128)S(1)}, s32[]{:T(128)}, s32[]{:T(128)}) %tuple.128), condition=%wide.region_10.11_spmd.clone, body=%wide.region_8.10_spmd.clone.sunk | while | flops 460034 | bytes 265308 | solution.py:110
  (1554 shorter events, 543.1 us)
Async XLA Ops:
  7.2 336.4 %all-reduce.11.cloned.1.call-start = ((), (), s32[]{:S(2)}) async-start(), calls=%async_computation.1 | async-start | bytes 196608
  8.8 9.3 collective-permute-start
  13.4 9.1 collective-permute-start.1
  25.3 14.3 %collective-permute-start.2 = (f32[3,32,12,2]{1,3,2,0:T(2,128)}, f32[3,32,12,2]{1,3,2,0:T(2,128)}, u32[]{:S(2)}, u32[]{:S(2)}) collective-permute-start(f32[3,32,12,2]{1,3,2,0:T(2,128)} %get-tuple-element.277), channel_id=1, source_target_pairs={{0,1},{1,2},{2,3},{3,4},{4,5},{5,6},{6,7},{8,9},{9,10},{10,11},{11... | collective-permute-start | bytes 27656 | tf_op jit(solution)/shard_map/ppermute | solution.py:16
  29.4 11.3 %collective-permute-start.3 = (f32[3,32,12,2]{1,3,2,0:T(2,128)}, f32[3,32,12,2]{1,3,2,0:T(2,128)}, u32[]{:S(2)}, u32[]{:S(2)}) collective-permute-start(f32[3,32,12,2]{1,3,2,0:T(2,128)} %get-tuple-element.276), channel_id=1, source_target_pairs={{1,0},{2,1},{3,2},{4,3},{5,4},{6,5},{7,6},{9,8},{10,9},{11,10},{12... | collective-permute-start | bytes 27656 | tf_op jit(solution)/shard_map/ppermute | solution.py:19
  46.1 7.0 collective-permute-start.5
  57.1 10.0 %collective-permute-start.6 = (f32[6,32,12,2]{1,3,2,0:T(2,128)S(1)}, f32[6,32,12,2]{1,3,2,0:T(2,128)}, u32[]{:S(2)}, u32[]{:S(2)}) collective-permute-start(f32[6,32,12,2]{1,3,2,0:T(2,128)S(1)} %copy.317), channel_id=1, source_target_pairs={{0,1},{1,2},{2,3},{3,4},{4,5},{5,6},{6,7},{8,9},{9,10},{10,11},{11... | collective-permute-start | bytes 55304 | tf_op jit(solution)/shard_map/ppermute | solution.py:16
  79.5 5.9 collective-permute-start.9
  88.5 7.0 collective-permute-start.10
  105.4 7.0 collective-permute-start.13
  116.1 10.2 %collective-permute-start.14 = (f32[6,32,12,2]{1,3,2,0:T(2,128)S(1)}, f32[6,32,12,2]{1,3,2,0:T(2,128)S(1)}, u32[]{:S(2)}, u32[]{:S(2)}) collective-permute-start(f32[6,32,12,2]{1,3,2,0:T(2,128)S(1)} %copy.329), channel_id=1, source_target_pairs={{0,1},{1,2},{2,3},{3,4},{4,5},{5,6},{6,7},{8,9},{9,10},{10,11},{11... | collective-permute-start | bytes 55304 | tf_op jit(solution)/shard_map/ppermute | solution.py:16
  135.6 11.6 %collective-permute-start.16 = (f32[3,32,2,128]{3,1,2,0:T(8,128)S(1)}, f32[3,32,2,128]{3,1,2,0:T(8,128)S(1)}, u32[]{:S(2)}, u32[]{:S(2)}) collective-permute-start(f32[3,32,2,128]{3,1,2,0:T(8,128)S(1)} %get-tuple-element.316), channel_id=1, source_target_pairs={{0,8},{8,16},{16,24},{24,32},{32,40},{40,48},{48,56},{56,64},{64,7... | collective-permute-start | bytes 294920 | tf_op jit(solution)/shard_map/ppermute | solution.py:16
  138.6 8.6 collective-permute-start.17
  149.7 6.7 collective-permute-start.18
  162.7 16.3 %collective-permute-start.20 = (f32[6,32,2,128]{3,1,2,0:T(8,128)S(1)}, f32[6,32,2,128]{3,1,2,0:T(8,128)S(1)}, u32[]{:S(2)}, u32[]{:S(2)}) collective-permute-start(f32[6,32,2,128]{3,1,2,0:T(8,128)S(1)} %get-tuple-element.294), channel_id=1, source_target_pairs={{0,8},{8,16},{16,24},{24,32},{32,40},{40,48},{48,56},{56,64},{64,7... | collective-permute-start | bytes 589832 | tf_op jit(solution)/shard_map/ppermute | solution.py:16
  168.8 10.2 %collective-permute-start.21 = (f32[6,32,2,128]{3,1,2,0:T(8,128)S(1)}, f32[6,32,2,128]{3,1,2,0:T(8,128)S(1)}, u32[]{:S(2)}, u32[]{:S(2)}) collective-permute-start(f32[6,32,2,128]{3,1,2,0:T(8,128)S(1)} %get-tuple-element.295), channel_id=1, source_target_pairs={{8,0},{16,8},{24,16},{32,24},{40,32},{48,40},{56,48},{64,56},{72,6... | collective-permute-start | bytes 589832 | tf_op jit(solution)/shard_map/ppermute | solution.py:19
  184.4 9.2 collective-permute-start.22
  201.1 11.8 %collective-permute-start.24 = (f32[3,32,2,128]{3,1,2,0:T(8,128)S(1)}, f32[3,32,2,128]{3,1,2,0:T(8,128)S(1)}, u32[]{:S(2)}, u32[]{:S(2)}) collective-permute-start(f32[3,32,2,128]{3,1,2,0:T(8,128)S(1)} %get-tuple-element.312), channel_id=1, source_target_pairs={{0,8},{8,16},{16,24},{24,32},{32,40},{40,48},{48,56},{56,64},{64,7... | collective-permute-start | bytes 294920 | tf_op jit(solution)/shard_map/ppermute | solution.py:16
  206.2 6.8 collective-permute-start.25
  213.5 6.8 collective-permute-start.26
  225.2 8.4 collective-permute-start.28
  230.0 7.0 collective-permute-start.29
  240.7 8.7 collective-permute-start.30
  262.7 214.0 %all-gather.3.cloned.1.call-start = ((), (), s32[]{:S(2)}) async-start(), calls=%async_computation | async-start | bytes 16842752 | tf_op jit(solution)/shard_map/all_gather | solution.py:152
  (54 other events, 253.5 us)
Sparse Core Ops, SparseCore 0:
  262.8 80.7 all-reduce.10
  348.4 128.2 all-gather.2
